TPU v7x, 128 devices: a whole 4x4x4 slice. The times are simulated.
128 devices in a mesh: expert: 8 (over z, core), fsdp: 16 (over y, x).
Axes of the slice: x: 4, y: 4, z: 4, core: 2. Of those that a mesh axis runs over, the one named last changes fastest.
Arguments:
- tokens: bfloat16 [32768, 2048], P(('expert', 'fsdp')), may hold values from -6 to 6
- expert_ids: int32 [32768, 6], P(('expert', 'fsdp')), may hold values from 0 to 63, as said below
- gate_vals: bfloat16 [32768, 6], P(('expert', 'fsdp')), may hold values from 0.099609375 to 1
- w_gate: bfloat16 [8, 2048, 1408], P('expert', 'fsdp'), may hold values from -0.125 to 0.125
- w_up: bfloat16 [8, 2048, 1408], P('expert', 'fsdp'), may hold values from -0.125 to 0.125
- w_down: bfloat16 [8, 2048, 1408], P('expert', 'fsdp'), may hold values from -0.15625 to 0.15625
- cotangent: bfloat16 [32768, 2048], P(('expert', 'fsdp')), may hold values from -6 to 6
Outputs:
- output: bfloat16 [32768, 2048], P(('expert', 'fsdp'))
- grad_tokens: bfloat16 [32768, 2048], P(('expert', 'fsdp'))
- grad_gates: float32 [32768, 6], P(('expert', 'fsdp'))
- grad_w_gate: float32 [8, 2048, 1408], P('expert', 'fsdp')
- grad_w_up: float32 [8, 2048, 1408], P('expert', 'fsdp')
- grad_w_down: float32 [8, 2048, 1408], P('expert', 'fsdp')
Inputs may be any that keep to these rules, and one draw needn't show every extreme that they name: `expert_ids`: each row names 6 different experts. Among the tokens of one device at most 48 name any one expert whose number modulo 8 is below 1. On every device some such expert is named by exactly 48 of its tokens, and for every column one such expert is named by exactly 48 tokens of every device of that column.
All inputs are finite; a program needn't handle non-finite values.
Results may differ from a plain program's by a relative error of at most 0.013.
Values may be sent and summed in bfloat16 or wider, within the bound.
No kernel may reach another device: no remote copies, remote signals or barrier semaphores. Data moves between devices by JAX's collectives and lax.ppermute only.
A program may use at most 128 MiB of HBM per device.

v0:
```python
import jax
import jax.numpy as jnp
from jax import lax
from jax.sharding import PartitionSpec as P

EXPERTS = 64
TOP = 6
WAVE = 1
MOST = 48


def slot_tables(expert_ids, groups):
    per_index = EXPERTS // groups
    window = WAVE * groups
    tok_count = expert_ids.shape[0]
    flat_ids = expert_ids.reshape(-1)
    local_index = flat_ids % per_index
    is_live = local_index < WAVE
    window_slot = jnp.where(is_live, flat_ids // per_index * WAVE + local_index, window)
    onehot = (window_slot[:, None] == jnp.arange(window, dtype=jnp.int32)[None, :]).astype(
        jnp.int32
    )
    rank_in = jnp.sum((jnp.cumsum(onehot, axis=0) - 1) * onehot, axis=1)
    target = jnp.where(is_live, window_slot * MOST + rank_in, window * MOST)
    slot_ids = jnp.arange(tok_count * TOP, dtype=jnp.int32)
    source = (
        jnp.full((window * MOST,), tok_count * TOP, jnp.int32).at[target].set(slot_ids, mode="drop")
    )
    return (target, source)


def on_device(tokens, expert_ids, gate_vals, w_gate, w_up, w_down, cotangent):
    groups = lax.axis_size("expert")
    tok_count, model_width = tokens.shape
    target, source = slot_tables(expert_ids, groups)
    token_of = source // TOP
    zero_row = jnp.zeros((1, model_width), jnp.bfloat16)
    tokens_pad = jnp.concatenate([tokens, zero_row], axis=0)
    cot_pad = jnp.concatenate([cotangent, zero_row], axis=0)
    gate_pad = jnp.concatenate([gate_vals.reshape(-1), jnp.zeros((1,), jnp.bfloat16)], axis=0)
    send_rows = tokens_pad[token_of].reshape(groups, WAVE * MOST, model_width)
    arrived = lax.all_to_all(send_rows, "expert", split_axis=0, concat_axis=0, tiled=True)
    rows_in = arrived.reshape(groups, WAVE, MOST, model_width)
    full_gate, full_up, full_down = (
        lax.all_gather(w_gate, "fsdp", axis=1, tiled=True),
        lax.all_gather(w_up, "fsdp", axis=1, tiled=True),
        lax.all_gather(w_down, "fsdp", axis=1, tiled=True),
    )
    gate_pre = jnp.einsum("skmd,kdf->skmf", rows_in, full_gate, preferred_element_type=jnp.float32)
    up_pre = jnp.einsum("skmd,kdf->skmf", rows_in, full_up, preferred_element_type=jnp.float32)
    sigmoid_g = jax.nn.sigmoid(gate_pre)
    hidden = (gate_pre * sigmoid_g * up_pre).astype(jnp.bfloat16)
    expert_out = jnp.einsum(
        "skmf,kdf->skmd", hidden, full_down, preferred_element_type=jnp.float32
    ).astype(jnp.bfloat16)
    returned = lax.all_to_all(
        expert_out.reshape(groups, WAVE * MOST, model_width),
        "expert",
        split_axis=0,
        concat_axis=0,
        tiled=True,
    )
    back_pad = jnp.concatenate([returned.reshape(-1, model_width), zero_row], axis=0)
    slot_out = back_pad[target].reshape(tok_count, TOP, model_width).astype(jnp.float32)
    output = jnp.sum(gate_vals.astype(jnp.float32)[:, :, None] * slot_out, axis=1).astype(
        jnp.bfloat16
    )
    grad_gates = jnp.sum(cotangent.astype(jnp.float32)[:, None, :] * slot_out, axis=2)
    gate_rows = gate_pad[source].astype(jnp.float32)
    send_grad = (gate_rows[:, None] * cot_pad[token_of].astype(jnp.float32)).astype(jnp.bfloat16)
    grad_in = lax.all_to_all(
        send_grad.reshape(groups, WAVE * MOST, model_width),
        "expert",
        split_axis=0,
        concat_axis=0,
        tiled=True,
    )
    out_grad = grad_in.reshape(groups, WAVE, MOST, model_width)
    hidden_grad = jnp.einsum(
        "skmd,kdf->skmf", out_grad, full_down, preferred_element_type=jnp.float32
    )
    gate_grad = (hidden_grad * up_pre * sigmoid_g * (1.0 + gate_pre * (1.0 - sigmoid_g))).astype(
        jnp.bfloat16
    )
    up_grad = (hidden_grad * gate_pre * sigmoid_g).astype(jnp.bfloat16)
    row_grad = (
        jnp.einsum("skmf,kdf->skmd", gate_grad, full_gate, preferred_element_type=jnp.float32)
        + jnp.einsum("skmf,kdf->skmd", up_grad, full_up, preferred_element_type=jnp.float32)
    ).astype(jnp.bfloat16)
    grads_home = lax.all_to_all(
        row_grad.reshape(groups, WAVE * MOST, model_width),
        "expert",
        split_axis=0,
        concat_axis=0,
        tiled=True,
    )
    grads_pad = jnp.concatenate([grads_home.reshape(-1, model_width), zero_row], axis=0)
    grad_tokens = jnp.sum(
        grads_pad[target].reshape(tok_count, TOP, model_width).astype(jnp.float32), axis=1
    ).astype(jnp.bfloat16)
    term_gate = jnp.einsum("skmd,skmf->kdf", rows_in, gate_grad, preferred_element_type=jnp.float32)
    term_up = jnp.einsum("skmd,skmf->kdf", rows_in, up_grad, preferred_element_type=jnp.float32)
    term_down = jnp.einsum("skmd,skmf->kdf", out_grad, hidden, preferred_element_type=jnp.float32)
    grad_w_gate, grad_w_up, grad_w_down = (
        lax.psum_scatter(
            term_gate.astype(jnp.bfloat16), "fsdp", scatter_dimension=1, tiled=True
        ).astype(jnp.float32),
        lax.psum_scatter(
            term_up.astype(jnp.bfloat16), "fsdp", scatter_dimension=1, tiled=True
        ).astype(jnp.float32),
        lax.psum_scatter(
            term_down.astype(jnp.bfloat16), "fsdp", scatter_dimension=1, tiled=True
        ).astype(jnp.float32),
    )
    return (output, grad_tokens, grad_gates, grad_w_gate, grad_w_up, grad_w_down)


def solution(mesh):
    placed = (
        P(("expert", "fsdp"), None),
        P(("expert", "fsdp"), None),
        P(("expert", "fsdp"), None),
        P("expert", "fsdp", None),
        P("expert", "fsdp", None),
        P("expert", "fsdp", None),
        P(("expert", "fsdp"), None),
    )
    return jax.shard_map(
        on_device,
        mesh=mesh,
        in_specs=placed,
        out_specs=(
            P(("expert", "fsdp"), None),
            P(("expert", "fsdp"), None),
            P(("expert", "fsdp"), None),
            P("expert", "fsdp", None),
            P("expert", "fsdp", None),
            P("expert", "fsdp", None),
        ),
        check_vma=False,
    )
```

profile of v0, /device:TPU:0, one launch (start us, length us, event | category | flops | bytes accessed | tf_op | source)
XLA Modules:
  0.0 461.0 jit_solution(18036882781366785138)
XLA Ops:
  7.2 0.7 all-gather.8.cloned.1.call-update
  8.0 0.7 all-gather.6.cloned.1.call-update
  9.4 0.8 copy.20
  10.7 0.8 copy.23
  11.7 2.3 reduce-window.6
  14.7 6.2 %scatter_custom_fusion = s32[384]{0:T(512)S(1)} fusion(s32[1536]{0:T(1024)S(1)} %get-tuple-element.15, s32[1536]{0:T(1024)S(1)} %iota.11, s32[]{:T(128)} %constant.52.clone.1), kind=kCustom, calls=%fused_computation.94 | custom fusion | bytes 1540 | tf_op jit(solution)/shard_map/scatter | solution.py:27
  20.9 2.8 gather_fusion.2
  23.9 2.5 gather_fusion.3
  26.4 1.5 fusion.15
  27.9 5.4 %all-to-all-start.2 = ((bf16[8,48,2048]{2,1,0:T(8,128)(2,1)}), bf16[8,48,2048]{2,1,0:T(8,128)(2,1)S(1)}, u32[]{:S(2)}, u32[]{:S(2)}) async-start(bf16[8,48,2048]{2,1,0:T(8,128)(2,1)} %fusion.15), calls=%async_computation.2 | async-start | bytes 3145728 | tf_op jit(solution)/shard_map/all_to_all | solution.py:71
  33.3 1.3 concatenate.15
  34.6 3.1 gather_fusion
  37.7 17.1 %all-to-all-done.2 = bf16[8,48,2048]{2,1,0:T(8,128)(2,1)S(1)} async-done(((bf16[8,48,2048]{2,1,0:T(8,128)(2,1)}), bf16[8,48,2048]{2,1,0:T(8,128)(2,1)S(1)}, u32[]{:S(2)}, u32[]{:S(2)}) %all-to-all-start.2) | async-done | bytes 1572896 | tf_op jit(solution)/shard_map/all_to_all | solution.py:71
  54.9 3.6 all-to-all-start
  58.5 12.8 %all-gather.8.cloned.1.call-done = bf16[1,2048,1408]{2,1,0:T(8,128)(2,1)} async-done(((bf16[1,128,1408]{2,1,0:T(8,128)(2,1)}), bf16[1,2048,1408]{2,1,0:T(8,128)(2,1)}) %all-gather.8.cloned.1.call-update) | async-done | bytes 5767184 | tf_op jit(solution)/shard_map/all_gather | solution.py:47
  71.4 6.6 %fusion.22 = f32[8,1,48,1408]{3,2,0,1:T(8,128)} fusion(bf16[8,48,2048]{2,1,0:T(8,128)(2,1)S(1)} %all-to-all-done.2, bf16[1,2048,1408]{2,1,0:T(8,128)(2,1)} %all-gather.8.cloned.1.call-done), kind=kOutput, calls=%fused_computation.31 | convolution fusion | flops 2214592512 | bytes 9502720 | tf_op jit(solution)/shard_map/skmd,kdf->skmf/dot_general | solution.py:79
  78.0 2.0 all-to-all-done
  80.0 52.0 %all-gather.6.cloned.1.call-done = bf16[1,2048,1408]{2,1,0:T(8,128)(2,1)} async-done(((bf16[1,128,1408]{2,1,0:T(8,128)(2,1)}), bf16[1,2048,1408]{2,1,0:T(8,128)(2,1)}) %all-gather.6.cloned.1.call-update) | async-done | bytes 5767184 | tf_op jit(solution)/shard_map/all_gather | solution.py:46
  132.0 6.6 %fusion.19 = f32[8,1,48,1408]{3,2,0,1:T(8,128)} fusion(bf16[8,48,2048]{2,1,0:T(8,128)(2,1)S(1)} %all-to-all-done, bf16[1,2048,1408]{2,1,0:T(8,128)(2,1)} %all-gather.6.cloned.1.call-done), kind=kOutput, calls=%fused_computation.30 | convolution fusion | flops 2214592512 | bytes 9502720 | tf_op jit(solution)/shard_map/skmd,kdf->skmf/dot_general | solution.py:50
  138.6 54.0 %all-gather.4.cloned.1.call-done = bf16[1,2048,1408]{2,1,0:T(8,128)(2,1)} async-done(((bf16[1,128,1408]{2,1,0:T(8,128)(2,1)}), bf16[1,2048,1408]{2,1,0:T(8,128)(2,1)}) %all-gather.4.cloned.1.call-update) | async-done | bytes 5767184 | tf_op jit(solution)/shard_map/all_gather | solution.py:45
  192.6 7.9 %multiply_convert_fusion.1 = (bf16[8,1,48,1408]{3,2,0,1:T(8,128)(2,1)}, bf16[8,1,48,1408]{3,2,0,1:T(8,128)(2,1)S(1)}, bf16[8,1,48,1408]{3,2,0,1:T(8,128)(2,1)}) fusion(f32[8,1,48,1408]{3,2,0,1:T(8,128)} %fusion.22, f32[8,1,48,1408]{3,2,0,1:T(8,128)} %fusion.19, bf16[8,48,2048]{2,1,0:T(8,128)(2,1)S(1)} %all-to-all-done, ...), kind=kOutput, calls=%fused_computation.34 | convolution fusion | flops 2223243264 | bytes 14909440 | tf_op jit(solution)/shard_map/skmd,kdf->skmf/dot_general | solution.py:49
  200.5 1.0 copy-done.5
  201.5 5.2 %fusion.2 = bf16[1,2048,1408]{2,1,0:T(8,128)(2,1)} fusion(bf16[8,48,2048]{2,1,0:T(8,128)(2,1)S(1)} %all-to-all-done.2, bf16[8,1,48,1408]{3,2,0,1:T(8,128)(2,1)S(1)} %get-tuple-element.17), kind=kOutput, calls=%fused_computation.13 | convolution fusion | flops 2217476096 | bytes 8421376 | tf_op jit(solution)/shard_map/skmd,skmf->kdf/dot_general | solution.py:103
  206.9 1.0 copy-done.7
  207.9 5.1 %fusion = bf16[1,2048,1408]{2,1,0:T(8,128)(2,1)} fusion(bf16[8,48,2048]{2,1,0:T(8,128)(2,1)S(1)} %all-to-all-done, bf16[8,1,48,1408]{3,2,0,1:T(8,128)(2,1)S(1)} %copy-done.7), kind=kOutput, calls=%fused_computation.11 | convolution fusion | flops 2217476096 | bytes 8421376 | tf_op jit(solution)/shard_map/skmd,skmf->kdf/dot_general | solution.py:101
  213.1 1.2 copy-done.4
  214.3 5.1 %fusion.1 = bf16[1,2048,1408]{2,1,0:T(8,128)(2,1)} fusion(bf16[8,48,2048]{2,1,0:T(8,128)(2,1)S(1)} %all-to-all-done, bf16[8,1,48,1408]{3,2,0,1:T(8,128)(2,1)S(1)} %copy-done.4), kind=kOutput, calls=%fused_computation.12 | convolution fusion | flops 2217476096 | bytes 8421376 | tf_op jit(solution)/shard_map/skmd,skmf->kdf/dot_general | solution.py:102
  219.4 1.2 copy-done.6
  220.6 7.8 %fusion.27 = bf16[8,48,2048]{2,1,0:T(8,128)(2,1)} fusion(bf16[1,2048,1408]{2,1,0:T(8,128)(2,1)} %all-gather.8.cloned.1.call-done, bf16[8,1,48,1408]{3,2,0,1:T(8,128)(2,1)S(1)} %copy-done.6), kind=kOutput, calls=%fused_computation.32 | convolution fusion | flops 2215378944 | bytes 8421376 | tf_op jit(solution)/shard_map/skmf,kdf->skmd/dot_general | solution.py:53
  228.4 4.6 all-to-all-start.1
  232.9 5.2 %fusion.7 = f32[8,48,2048]{2,1,0:T(8,128)S(1)} fusion(bf16[1,2048,1408]{2,1,0:T(8,128)(2,1)} %all-gather.6.cloned.1.call-done, bf16[8,1,48,1408]{3,2,0,1:T(8,128)(2,1)} %get-tuple-element.18), kind=kOutput, calls=%fused_computation.18 | convolution fusion | flops 2214592512 | bytes 9994240 | tf_op jit(solution)/shard_map/skmf,kdf->skmd/dot_general | solution.py:88
  238.2 3.8 add_convert_fusion
  242.0 12.5 %all-to-all-done.1 = bf16[8,48,2048]{2,1,0:T(8,128)(2,1)S(1)} async-done(((bf16[8,48,2048]{2,1,0:T(8,128)(2,1)}), bf16[8,48,2048]{2,1,0:T(8,128)(2,1)S(1)}, u32[]{:S(2)}, u32[]{:S(2)}) %all-to-all-start.1) | async-done | bytes 1572896 | tf_op jit(solution)/shard_map/all_to_all | solution.py:56
  254.5 4.3 all-to-all-start.3
  259.0 1.6 convert_element_type.110
  260.8 19.6 %all-to-all-done.3 = bf16[8,48,2048]{2,1,0:T(8,128)(2,1)} async-done(((bf16[8,48,2048]{2,1,0:T(8,128)(2,1)}), bf16[8,48,2048]{2,1,0:T(8,128)(2,1)}, u32[]{:S(2)}, u32[]{:S(2)}) %all-to-all-start.3) | async-done | bytes 1572896 | tf_op jit(solution)/shard_map/all_to_all | solution.py:90
  280.4 1.5 concatenate.19
  281.9 7.1 %gather_fusion.4 = bf16[1536,2048]{1,0:T(8,128)(2,1)} fusion(bf16[385,2048]{1,0:T(8,128)(2,1)S(1)} %concatenate.19, s32[2048]{0:T(1024)S(1)} %pad_clamp_fusion), kind=kCustom, calls=%fused_computation.4 | custom fusion | bytes 12589056 | tf_op jit(solution)/shard_map/gather | solution.py:99
  289.0 11.0 %reshape.325 = bf16[256,6,2048]{2,1,0:T(8,128)(2,1)} reshape(bf16[1536,2048]{1,0:T(8,128)(2,1)} %gather_fusion.4) | data formatting | bytes 12582912 | tf_op jit(solution)/shard_map/reshape | solution.py:99
  300.0 9.7 %reduce_sum.44 = bf16[256,2048]{1,0:T(8,128)(2,1)} reduce(bf16[256,6,2048]{2,1,0:T(8,128)(2,1)} %reshape.325, bf16[]{:T(256)} %constant.31.clone.1), dimensions={1}, to_apply=%region_5.6 | reduce | flops 2621440 | bytes 7340034 | tf_op jit(solution)/shard_map/reduce_sum | solution.py:98
  309.8 7.1 %gather_fusion.1 = bf16[1536,2048]{1,0:T(8,128)(2,1)} fusion(bf16[385,2048]{1,0:T(8,128)(2,1)S(1)} %concatenate.16, s32[2048]{0:T(1024)S(1)} %pad_clamp_fusion), kind=kCustom, calls=%fused_computation.1 | custom fusion | bytes 12589056 | tf_op jit(solution)/shard_map/gather | solution.py:64
  316.9 12.0 %reshape.326 = f32[256,6,2048]{2,1,0:T(8,128)} reshape(bf16[1536,2048]{1,0:T(8,128)(2,1)} %gather_fusion.1) | data formatting | bytes 18874368 | tf_op jit(solution)/shard_map/convert_element_type | solution.py:64
  328.9 11.9 %multiply_reduce_fusion = (f32[256,6]{1,0:T(8,128)S(1)}, bf16[256,2048]{1,0:T(8,128)(2,1)}) fusion(f32[256,6,2048]{2,1,0:T(8,128)} %reshape.326, f32[256,2048]{1,0:T(8,128)S(1)} %copy-done, f32[256,6]{1,0:T(8,128)S(1)} %copy.19), kind=kLoop, calls=%fused_computation.6 | loop fusion | flops 12057088 | bytes 15740928 | tf_op jit(solution)/shard_map/reduce_sum | solution.py:68
  341.5 1.9 convert_element_type.119
  343.4 26.1 %reduce-scatter.4.cloned.1.call-done = bf16[1,128,1408]{2,1,0:T(8,128)(2,1)} async-done(((bf16[1,2048,1408]{2,1,0:T(8,128)(2,1)}), bf16[1,128,1408]{2,1,0:T(8,128)(2,1)}) %reduce-scatter.4.cloned.1.call-update) | async-done | bytes 360464 | tf_op jit(solution)/shard_map/reduce_scatter | solution.py:105
  369.5 1.9 convert_element_type.113
  371.4 80.9 %reduce-scatter.6.cloned.1.call-done = bf16[1,128,1408]{2,1,0:T(8,128)(2,1)} async-done(((bf16[1,2048,1408]{2,1,0:T(8,128)(2,1)}), bf16[1,128,1408]{2,1,0:T(8,128)(2,1)}) %reduce-scatter.6.cloned.1.call-update) | async-done | bytes 360464 | tf_op jit(solution)/shard_map/reduce_scatter | solution.py:108
  452.3 1.9 convert_element_type.116
  (52 shorter events, 3.7 us)
Async XLA Ops:
  7.2 16.6 %copy-start.1 = (bf16[256,2048]{1,0:T(8,128)(2,1)S(1)}, bf16[256,2048]{1,0:T(8,128)(2,1)}, u32[]{:S(2)}) copy-start(bf16[256,2048]{1,0:T(8,128)(2,1)} %param.13) | copy-start | bytes 3145732
  7.2 64.2 %all-gather.8.cloned.1.call-start = ((), (), s32[]{:S(2)}) async-start(), calls=%async_computation.9 | async-start | bytes 6127616 | tf_op jit(solution)/shard_map/all_gather | solution.py:47
  7.9 124.1 %all-gather.6.cloned.1.call-start = ((), (), s32[]{:S(2)}) async-start(), calls=%async_computation.8 | async-start | bytes 6127616 | tf_op jit(solution)/shard_map/all_gather | solution.py:46
  8.7 184.0 %all-gather.4.cloned.1.call-start = ((), (), s32[]{:S(2)}) async-start(), calls=%async_computation.7 | async-start | bytes 6127616 | tf_op jit(solution)/shard_map/all_gather | solution.py:45
  27.9 27.0 %all-to-all-start.2 = ((bf16[8,48,2048]{2,1,0:T(8,128)(2,1)}), bf16[8,48,2048]{2,1,0:T(8,128)(2,1)S(1)}, u32[]{:S(2)}, u32[]{:S(2)}) async-start(bf16[8,48,2048]{2,1,0:T(8,128)(2,1)} %fusion.15), calls=%async_computation.2 | async-start | bytes 3145728 | tf_op jit(solution)/shard_map/all_to_all | solution.py:71
  54.9 25.1 %all-to-all-start = ((bf16[8,48,2048]{2,1,0:T(8,128)(2,1)}), bf16[8,48,2048]{2,1,0:T(8,128)(2,1)S(1)}, u32[]{:S(2)}, u32[]{:S(2)}) async-start(bf16[8,48,2048]{2,1,0:T(8,128)(2,1)} %bitcast.1), calls=%async_computation | async-start | bytes 3145728 | tf_op jit(solution)/shard_map/all_to_all | solution.py:42
  58.5 283.0 %reduce-scatter.8.cloned.1.call-start = ((), (), s32[]{:S(2)}) async-start(), calls=%async_computation.12 | async-start | bytes 6127616 | tf_op jit(solution)/shard_map/reduce_scatter | solution.py:111
  200.5 1.0 copy-start.5
  206.7 1.2 copy-start.7
  206.7 162.8 %reduce-scatter.4.cloned.1.call-start = ((), (), s32[]{:S(2)}) async-start(), calls=%async_computation.10 | async-start | bytes 6127616 | tf_op jit(solution)/shard_map/reduce_scatter | solution.py:105
  213.0 1.2 copy-start.4
  213.1 239.2 %reduce-scatter.6.cloned.1.call-start = ((), (), s32[]{:S(2)}) async-start(), calls=%async_computation.11 | async-start | bytes 6127616 | tf_op jit(solution)/shard_map/reduce_scatter | solution.py:108
  219.4 1.2 copy-start.6
  228.4 9.8 %slice-start = ((s8[5767168]{0:T(1024)(128)(4,1)}), s8[1572864]{0:T(1024)(128)(4,1)S(1)}, s32[]{:S(2)}) async-start(s8[5767168]{0:T(1024)(128)(4,1)} %bitcast.111), calls=%async_computation.13 | async-start | bytes 3145728
  228.4 26.1 %all-to-all-start.1 = ((bf16[8,48,2048]{2,1,0:T(8,128)(2,1)}), bf16[8,48,2048]{2,1,0:T(8,128)(2,1)S(1)}, u32[]{:S(2)}, u32[]{:S(2)}) async-start(bf16[8,48,2048]{2,1,0:T(8,128)(2,1)} %fusion.27), calls=%async_computation.1 | async-start | bytes 3145728 | tf_op jit(solution)/shard_map/all_to_all | solution.py:56
  232.9 5.2 %slice-start.1 = ((s8[5767168]{0:T(1024)(128)(4,1)}), s8[4194304]{0:T(1024)(128)(4,1)S(1)}, s32[]{:S(2)}) async-start(s8[5767168]{0:T(1024)(128)(4,1)} %bitcast.111), calls=%async_computation.14 | async-start | bytes 8388608
  232.9 5.2 %copy-start.8 = (bf16[8,1,48,1408]{3,2,0,1:T(8,128)(2,1)S(1)}, bf16[8,1,48,1408]{3,2,0,1:T(8,128)(2,1)}, u32[]{:S(2)}) copy-start(bf16[8,1,48,1408]{3,2,0,1:T(8,128)(2,1)} %get-tuple-element.16) | copy-start | bytes 3244036
  242.0 16.8 %copy-start.3 = (bf16[256,6]{0,1:T(8,128)(2,1)S(1)}, bf16[256,6]{0,1:T(8,128)(2,1)}, u32[]{:S(2)}) copy-start(bf16[256,6]{0,1:T(8,128)(2,1)} %param.9) | copy-start | bytes 9220
  242.0 16.9 %copy-start.2 = (bf16[256,2048]{1,0:T(8,128)(2,1)S(1)}, bf16[256,2048]{1,0:T(8,128)(2,1)}, u32[]{:S(2)}) copy-start(bf16[256,2048]{1,0:T(8,128)(2,1)} %param.13) | copy-start | bytes 3145732
  254.5 25.9 %all-to-all-start.3 = ((bf16[8,48,2048]{2,1,0:T(8,128)(2,1)}), bf16[8,48,2048]{2,1,0:T(8,128)(2,1)}, u32[]{:S(2)}, u32[]{:S(2)}) async-start(bf16[8,48,2048]{2,1,0:T(8,128)(2,1)} %add_convert_fusion), calls=%async_computation.3 | async-start | bytes 3145728 | tf_op jit(solution)/shard_map/all_to_all | solution.py:90
  316.9 12.0 %copy-start = (f32[256,2048]{1,0:T(8,128)S(1)}, f32[256,2048]{1,0:T(8,128)}, u32[]{:S(2)}) copy-start(f32[256,2048]{1,0:T(8,128)} %convert_element_type.110) | copy-start | bytes 6291460
Sparse Core Ops, SparseCore 0:
  10.1 61.1 all-gather.7
  73.5 58.4 all-gather.5
  134.1 58.4 all-gather.3
  206.8 79.7 reduce-scatter.7
  289.8 79.5 reduce-scatter.3
  372.7 79.5 reduce-scatter.5
where the time goes:
time: 463 us; the launch traced here: 461 us
  waiting for transfers between devices  279 us (60%)
  local copies, waits for them, and re-layouts  62.6 us (14%)
  matrix products  53.3 us (12%)
  other arithmetic  33.2 us (7%)
  starting transfers between devices  18.3 us (4%)
  between operations  14.4 us (3%)
    reduce_scatter x1, waiting for transfers between devices, on_device(): lax.psum_scatter(term_up.astype(jnp.bfloat16), 'fsdp', scatter_dimension=...  80.9 us
    all_gather x1, waiting for transfers between devices, on_device(): lax.all_gather(w_gate, 'fsdp', axis=1, tiled=True)  54 us
    all_gather x1, waiting for transfers between devices, on_device(): lax.all_gather(w_up, 'fsdp', axis=1, tiled=True)  52 us
    reduce_scatter x1, waiting for transfers between devices, on_device(): lax.psum_scatter(term_gate.astype(jnp.bfloat16), 'fsdp', scatter_dimensio...  26.1 us
    all_to_all x1, waiting for transfers between devices, on_device(): lax.all_to_all(row_grad.reshape(groups, WAVE * MOST, model_width), 'exper...  19.6 us
    all_to_all x1, waiting for transfers between devices, on_device(): lax.all_to_all(send_grad.reshape(groups, WAVE * MOST, model_width), 'expe...  17.1 us
    all_gather x1, waiting for transfers between devices, on_device(): lax.all_gather(w_down, 'fsdp', axis=1, tiled=True)  12.8 us
    all_to_all x1, waiting for transfers between devices, on_device(): lax.all_to_all(expert_out.reshape(groups, WAVE * MOST, model_width), 'exp...  12.5 us
  transfers between devices with their start and end apart: 10, of which 9 were waited for; matrix products, arithmetic and copies ran while one was open for 28% of the time, Pallas kernels for 0%

commit v1 on v0

--- a/solution.py
+++ b/solution.py
@@ -7,6 +7,11 @@
 TOP = 6
 WAVE = 1
 MOST = 48
+
+
+def gather_by_exchange(shard, axis, dim):
+    copies = jnp.concatenate([shard] * lax.axis_size(axis), axis=dim)
+    return lax.all_to_all(copies, axis, dim, dim, tiled=True)
 
 
 def slot_tables(expert_ids, groups):
@@ -42,7 +47,7 @@
     arrived = lax.all_to_all(send_rows, "expert", split_axis=0, concat_axis=0, tiled=True)
     rows_in = arrived.reshape(groups, WAVE, MOST, model_width)
     full_gate, full_up, full_down = (
-        lax.all_gather(w_gate, "fsdp", axis=1, tiled=True),
+        gather_by_exchange(w_gate, "fsdp", 1),
         lax.all_gather(w_up, "fsdp", axis=1, tiled=True),
         lax.all_gather(w_down, "fsdp", axis=1, tiled=True),
     )

time: 463 us -> 583 us (1.26); the launches traced: 461 us -> 572 us
  other arithmetic: 33.2 us -> 159 us
  waiting for transfers between devices: 279 us -> 212 us
  local copies, waits for them, and re-layouts: 62.6 us -> 100 us
  matrix products: 53.3 us -> 62.1 us
  starting transfers between devices: 18.3 us -> 25 us
    unnamed x2 -> x3, other arithmetic: 0.09 us -> 124 us
    all_to_all x0 -> x1, waiting for transfers between devices: none -> 72.6 us  [gather_by_exchange(): return lax.all_to_all(copies, axis, dim, dim, tiled=True)]
    all_gather x1 -> x0, waiting for transfers between devices: 54 us -> none  [on_device(): lax.all_gather(w_gate, 'fsdp', axis=1, tiled=True)]
    all_gather x1, waiting for transfers between devices: 52 us -> 0.01 us  [on_device(): lax.all_gather(w_up, 'fsdp', axis=1, tiled=True)]
    unnamed x25 -> x47, local copies, waits for them, and re-layouts: 6.7 us -> 45 us
    all_gather x1, waiting for transfers between devices: 12.8 us -> 0.01 us  [on_device(): lax.all_gather(w_down, 'fsdp', axis=1, tiled=True)]
    all_to_all x1, waiting for transfers between devices: 12.5 us -> 0.01 us  [on_device(): lax.all_to_all(expert_out.reshape(groups, WAVE * MOST, model_width), 'exp...]
    reduce_scatter x1, waiting for transfers between devices: 26.1 us -> 37.7 us  [on_device(): lax.psum_scatter(term_gate.astype(jnp.bfloat16), 'fsdp', scatter_dimensio...]
  transfers between devices with their start and end apart: 10 -> 10, of which waited for: 9 -> 6; matrix products, arithmetic and copies ran while one was open for 28% -> 52% of each run, Pallas kernels for 0% -> 0%
where the time goes in v1:
time: 583 us; the launch traced here: 572 us
  waiting for transfers between devices  212 us (36%)
  other arithmetic  159 us (27%)
  local copies, waits for them, and re-layouts  100 us (17%)
  matrix products  62.1 us (11%)
  starting transfers between devices  25 us (4%)
  between operations  14.4 us (2%)
    unnamed x3, other arithmetic  124 us
    reduce_scatter x1, waiting for transfers between devices, on_device(): lax.psum_scatter(term_up.astype(jnp.bfloat16), 'fsdp', scatter_dimension=...  80.6 us
    all_to_all x1, waiting for transfers between devices, gather_by_exchange(): return lax.all_to_all(copies, axis, dim, dim, tiled=True)  72.6 us
    unnamed x47, local copies, waits for them, and re-layouts  45 us
    reduce_scatter x1, waiting for transfers between devices, on_device(): lax.psum_scatter(term_gate.astype(jnp.bfloat16), 'fsdp', scatter_dimensio...  37.7 us
    all_to_all x1, waiting for transfers between devices, on_device(): lax.all_to_all(row_grad.reshape(groups, WAVE * MOST, model_width), 'exper...  13.5 us
    reduce_sum x1, other arithmetic, on_device(): jnp.sum(cotangent.astype(jnp.float32)[:, None, :] * slot_out, axis=2)  12 us
    convert_element_type x1, local copies, waits for them, and re-layouts, on_device(): back_pad[target].reshape(tok_count, TOP, model_width).astype(jnp.float32)  12 us
  transfers between devices with their start and end apart: 10, of which 6 were waited for; matrix products, arithmetic and copies ran while one was open for 52% of the time, Pallas kernels for 0%

profile of v1, /device:TPU:0, one launch (start us, length us, event | category | flops | bytes accessed | tf_op | source)
XLA Modules:
  0.0 572.4 jit_solution(3572169499040377126)
XLA Ops:
  7.2 0.7 all-gather.3.cloned.1.call-update
  8.0 0.7 all-gather.5.cloned.1.call-update
  8.7 1.5 constant_dynamic-update-slice_fusion.15
  10.2 1.6 constant_dynamic-update-slice_fusion.14
  11.8 1.6 constant_dynamic-update-slice_fusion.13
  21.4 4.3 copy-done.1
  26.3 124.2 %reduce.11 = bf16[2048,1408]{1,0:T(8,128)(2,1)} reduce(bf16[2048,1,1408]{2,1,0:T(2,128)(2,1)} %bitcast.120, bf16[]{:T(256)} %broadcast.343), dimensions={1}, to_apply=%bitcast.109.reduce_sub_computation | reduce | bytes 11534338
  150.5 11.3 %reshape.397 = bf16[16,2,90112]{2,1,0:T(2,128)(2,1)} reshape(bf16[2048,1408]{1,0:T(8,128)(2,1)} %reduce.11) | data formatting | bytes 11534336
  161.8 7.3 %all-to-all-start = ((bf16[16,2,90112]{2,1,0:T(2,128)(2,1)}), bf16[16,2,90112]{2,1,0:T(2,128)(2,1)}, u32[]{:S(2)}, u32[]{:S(2)}) async-start(bf16[16,2,90112]{2,1,0:T(2,128)(2,1)} %reshape.397), calls=%async_computation | async-start | bytes 11534336 | tf_op jit(solution)/shard_map/all_to_all | solution.py:14
  169.8 2.3 reduce-window.6
  172.9 6.2 %scatter_custom_fusion = s32[384]{0:T(512)S(1)} fusion(s32[1536]{0:T(1024)S(1)} %get-tuple-element.21, s32[1536]{0:T(1024)S(1)} %iota.11, s32[]{:T(128)} %constant.52.clone.1), kind=kCustom, calls=%fused_computation.114 | custom fusion | bytes 1540 | tf_op jit(solution)/shard_map/scatter | solution.py:32
  179.1 3.1 gather_fusion
  182.2 72.6 %all-to-all-done = bf16[16,2,90112]{2,1,0:T(2,128)(2,1)} async-done(((bf16[16,2,90112]{2,1,0:T(2,128)(2,1)}), bf16[16,2,90112]{2,1,0:T(2,128)(2,1)}, u32[]{:S(2)}, u32[]{:S(2)}) %all-to-all-start) | async-done | bytes 5767200 | tf_op jit(solution)/shard_map/all_to_all | solution.py:14
  254.8 5.3 all-to-all-start.1
  260.3 2.5 gather_fusion.3
  263.1 2.8 gather_fusion.2
  266.0 1.5 fusion.15
  267.5 13.8 %reshape.398 = bf16[2048,1,1408]{2,1,0:T(2,128)(2,1)} reshape(bf16[16,2,90112]{2,1,0:T(2,128)(2,1)} %all-to-all-done) | data formatting | bytes 11534336
  281.8 4.3 all-to-all-start.3
  286.4 8.7 %fusion.17 = f32[8,1,48,1408]{3,2,0,1:T(8,128)} fusion(bf16[8,48,2048]{2,1,0:T(8,128)(2,1)} %all-to-all-done.1, bf16[1,2048,1408]{2,0,1:T(2,128)(2,1)} %bitcast.121), kind=kOutput, calls=%fused_computation.30 | convolution fusion | flops 2214592512 | bytes 9502720 | tf_op jit(solution)/shard_map/skmd,kdf->skmf/dot_general | solution.py:54
  295.0 7.1 %fusion.20 = f32[8,1,48,1408]{3,2,0,1:T(8,128)} fusion(bf16[8,48,2048]{2,1,0:T(8,128)(2,1)} %all-to-all-done.1, bf16[1,2048,1408]{2,1,0:T(8,128)(2,1)} %all-gather.3.cloned.1.call-done), kind=kOutput, calls=%fused_computation.31 | convolution fusion | flops 2214592512 | bytes 9502720 | tf_op jit(solution)/shard_map/skmd,kdf->skmf/dot_general | solution.py:55
  302.1 5.5 all-to-all-done.3
  307.7 7.5 %multiply_convert_fusion = (bf16[8,1,48,1408]{3,2,0,1:T(8,128)(2,1)}, bf16[8,1,48,1408]{3,2,0,1:T(8,128)(2,1)}, bf16[8,1,48,1408]{3,2,0,1:T(8,128)(2,1)S(1)}) fusion(f32[8,1,48,1408]{3,2,0,1:T(8,128)} %fusion.17, f32[8,1,48,1408]{3,2,0,1:T(8,128)} %fusion.20, bf16[8,48,2048]{2,1,0:T(8,128)(2,1)S(1)} %all-to-all-done.3, ...), kind=kOutput, calls=%fused_computation.37 | convolution fusion | flops 2223243264 | bytes 14909440 | tf_op jit(solution)/shard_map/skmd,kdf->skmf/dot_general | solution.py:84
  315.2 5.1 fusion.2
  320.4 1.2 copy-done.10
  321.6 7.3 %fusion = bf16[1,2048,1408]{2,1,0:T(8,128)(2,1)} fusion(bf16[8,48,2048]{2,1,0:T(8,128)(2,1)} %all-to-all-done.1, bf16[8,1,48,1408]{3,2,0,1:T(8,128)(2,1)S(1)} %copy-done.10), kind=kOutput, calls=%fused_computation.11 | convolution fusion | flops 2217476096 | bytes 8421376 | tf_op jit(solution)/shard_map/skmd,skmf->kdf/dot_general | solution.py:106
  329.4 0.8 copy-done.8
  330.1 7.2 %fusion.1 = bf16[1,2048,1408]{2,1,0:T(8,128)(2,1)} fusion(bf16[8,48,2048]{2,1,0:T(8,128)(2,1)} %all-to-all-done.1, bf16[8,1,48,1408]{3,2,0,1:T(8,128)(2,1)S(1)} %copy-done.8), kind=kOutput, calls=%fused_computation.12 | convolution fusion | flops 2217476096 | bytes 8421376 | tf_op jit(solution)/shard_map/skmd,skmf->kdf/dot_general | solution.py:107
  337.4 7.3 %fusion.3 = f32[2048,8,48]{0,2,1:T(8,128)S(1)} fusion(bf16[1,2048,1408]{2,0,1:T(2,128)(2,1)} %bitcast.122, bf16[8,1,48,1408]{3,2,0,1:T(8,128)(2,1)} %get-tuple-element.23), kind=kOutput, calls=%fused_computation.14 | convolution fusion | flops 2214592512 | bytes 9994240 | tf_op jit(solution)/shard_map/skmf,kdf->skmd/dot_general | solution.py:92
  344.8 3.8 fusion.31
  348.6 3.6 all-to-all-start.4
  352.2 8.0 %fusion.28 = bf16[8,48,2048]{2,1,0:T(8,128)(2,1)} fusion(bf16[1,2048,1408]{2,1,0:T(8,128)(2,1)} %all-gather.5.cloned.1.call-done, bf16[8,1,48,1408]{3,2,0,1:T(8,128)(2,1)S(1)} %get-tuple-element.24), kind=kOutput, calls=%fused_computation.33 | convolution fusion | flops 2215378944 | bytes 8421376 | tf_op jit(solution)/shard_map/skmf,kdf->skmd/dot_general | solution.py:58
  360.1 13.5 %all-to-all-done.4 = bf16[8,48,2048]{2,1,0:T(8,128)(2,1)S(1)} async-done(((bf16[8,48,2048]{2,1,0:T(8,128)(2,1)}), bf16[8,48,2048]{2,1,0:T(8,128)(2,1)S(1)}, u32[]{:S(2)}, u32[]{:S(2)}) %all-to-all-start.4) | async-done | bytes 1572896 | tf_op jit(solution)/shard_map/all_to_all | solution.py:95
  373.7 3.8 all-to-all-start.2
  377.4 2.9 convert_element_type.115
  380.5 1.5 concatenate.23
  382.0 7.0 %gather_fusion.4 = bf16[1536,2048]{1,0:T(8,128)(2,1)} fusion(bf16[385,2048]{1,0:T(8,128)(2,1)S(1)} %concatenate.23, s32[2048]{0:T(1024)S(1)} %pad_clamp_fusion), kind=kCustom, calls=%fused_computation.4 | custom fusion | bytes 12589056 | tf_op jit(solution)/shard_map/gather | solution.py:104
  389.0 11.0 %reshape.330 = bf16[256,6,2048]{2,1,0:T(8,128)(2,1)} reshape(bf16[1536,2048]{1,0:T(8,128)(2,1)} %gather_fusion.4) | data formatting | bytes 12582912 | tf_op jit(solution)/shard_map/reshape | solution.py:104
  400.0 9.7 %reduce_sum.44 = bf16[256,2048]{1,0:T(8,128)(2,1)} reduce(bf16[256,6,2048]{2,1,0:T(8,128)(2,1)} %reshape.330, bf16[]{:T(256)} %constant.31.clone.1), dimensions={1}, to_apply=%region_5.6 | reduce | flops 2621440 | bytes 7340034 | tf_op jit(solution)/shard_map/reduce_sum | solution.py:103
  410.0 7.1 %gather_fusion.1 = bf16[1536,2048]{1,0:T(8,128)(2,1)} fusion(bf16[385,2048]{1,0:T(8,128)(2,1)S(1)} %concatenate.20, s32[2048]{0:T(1024)S(1)} %pad_clamp_fusion), kind=kCustom, calls=%fused_computation.1 | custom fusion | bytes 12589056 | tf_op jit(solution)/shard_map/gather | solution.py:69
  417.0 12.0 %reshape.331 = f32[256,6,2048]{2,1,0:T(8,128)} reshape(bf16[1536,2048]{1,0:T(8,128)(2,1)} %gather_fusion.1) | data formatting | bytes 18874368 | tf_op jit(solution)/shard_map/convert_element_type | solution.py:69
  429.0 12.0 %multiply_reduce_fusion = (f32[256,6]{1,0:T(8,128)S(1)}, bf16[256,2048]{1,0:T(8,128)(2,1)}) fusion(f32[256,6,2048]{2,1,0:T(8,128)} %reshape.331, f32[256,2048]{1,0:T(8,128)S(1)} %copy-done.2, f32[256,6]{1,0:T(8,128)S(1)} %copy.41), kind=kLoop, calls=%fused_computation.6 | loop fusion | flops 12057088 | bytes 15740928 | tf_op jit(solution)/shard_map/reduce_sum | solution.py:73
  441.0 0.7 copy.62
  441.7 1.9 convert_element_type.124
  443.6 37.7 %reduce-scatter.4.cloned.1.call-done = bf16[1,128,1408]{2,1,0:T(8,128)(2,1)} async-done(((bf16[1,2048,1408]{2,1,0:T(8,128)(2,1)}), bf16[1,128,1408]{2,1,0:T(8,128)(2,1)}) %reduce-scatter.4.cloned.1.call-update) | async-done | bytes 360464 | tf_op jit(solution)/shard_map/reduce_scatter | solution.py:110
  481.3 1.9 convert_element_type.118
  483.2 80.6 %reduce-scatter.6.cloned.1.call-done = bf16[1,128,1408]{2,1,0:T(8,128)(2,1)} async-done(((bf16[1,2048,1408]{2,1,0:T(8,128)(2,1)}), bf16[1,128,1408]{2,1,0:T(8,128)(2,1)}) %reduce-scatter.6.cloned.1.call-update) | async-done | bytes 360464 | tf_op jit(solution)/shard_map/reduce_scatter | solution.py:113
  563.8 1.9 convert_element_type.121
  (75 shorter events, 12.1 us)
Async XLA Ops:
  7.2 6.2 %copy-start = (bf16[1,128,1408]{2,1,0:T(8,128)(2,1)S(1)}, bf16[1,128,1408]{2,1,0:T(8,128)(2,1)}, u32[]{:S(2)}) copy-start(bf16[1,128,1408]{2,1,0:T(8,128)(2,1)} %param.10) | copy-start | bytes 1081348
  7.2 287.9 %all-gather.3.cloned.1.call-start = ((), (), s32[]{:S(2)}) async-start(), calls=%async_computation.8 | async-start | bytes 6127616 | tf_op jit(solution)/shard_map/all_gather | solution.py:51
  7.9 299.8 %all-gather.5.cloned.1.call-start = ((), (), s32[]{:S(2)}) async-start(), calls=%async_computation.9 | async-start | bytes 6127616 | tf_op jit(solution)/shard_map/all_gather | solution.py:52
  21.4 4.3 copy-start.1
  161.8 7.3 %copy-start.7 = (s32[256,6]{0,1:T(8,128)S(1)}, s32[256,6]{0,1:T(8,128)}, u32[]{:S(2)}) copy-start(s32[256,6]{0,1:T(8,128)} %param.8) | copy-start | bytes 18436
  161.8 10.7 %copy-start.5 = (bf16[256,2048]{1,0:T(8,128)(2,1)S(1)}, bf16[256,2048]{1,0:T(8,128)(2,1)}, u32[]{:S(2)}) copy-start(bf16[256,2048]{1,0:T(8,128)(2,1)} %param.7) | copy-start | bytes 3145732
  161.8 93.0 %all-to-all-start = ((bf16[16,2,90112]{2,1,0:T(2,128)(2,1)}), bf16[16,2,90112]{2,1,0:T(2,128)(2,1)}, u32[]{:S(2)}, u32[]{:S(2)}) async-start(bf16[16,2,90112]{2,1,0:T(2,128)(2,1)} %reshape.397), calls=%async_computation | async-start | bytes 11534336 | tf_op jit(solution)/shard_map/all_to_all | solution.py:14
  182.2 77.9 %copy-start.4 = (bf16[256,2048]{1,0:T(8,128)(2,1)S(1)}, bf16[256,2048]{1,0:T(8,128)(2,1)}, u32[]{:S(2)}) copy-start(bf16[256,2048]{1,0:T(8,128)(2,1)} %param.13) | copy-start | bytes 3145732
  254.8 27.0 %all-to-all-start.1 = ((bf16[8,48,2048]{2,1,0:T(8,128)(2,1)}), bf16[8,48,2048]{2,1,0:T(8,128)(2,1)}, u32[]{:S(2)}, u32[]{:S(2)}) async-start(bf16[8,48,2048]{2,1,0:T(8,128)(2,1)} %bitcast.1), calls=%async_computation.1 | async-start | bytes 3145728 | tf_op jit(solution)/shard_map/all_to_all | solution.py:47
  260.3 2.5 copy-start.6
  281.8 25.8 %all-to-all-start.3 = ((bf16[8,48,2048]{2,1,0:T(8,128)(2,1)}), bf16[8,48,2048]{2,1,0:T(8,128)(2,1)S(1)}, u32[]{:S(2)}, u32[]{:S(2)}) async-start(bf16[8,48,2048]{2,1,0:T(8,128)(2,1)} %fusion.15), calls=%async_computation.3 | async-start | bytes 3145728 | tf_op jit(solution)/shard_map/all_to_all | solution.py:76
  286.1 155.6 %reduce-scatter.8.cloned.1.call-start = ((), (), s32[]{:S(2)}) async-start(), calls=%async_computation.12 | async-start | bytes 6127616 | tf_op jit(solution)/shard_map/reduce_scatter | solution.py:116
  320.4 1.2 copy-start.10
  320.4 160.9 %reduce-scatter.4.cloned.1.call-start = ((), (), s32[]{:S(2)}) async-start(), calls=%async_computation.10 | async-start | bytes 6127616 | tf_op jit(solution)/shard_map/reduce_scatter | solution.py:110
  328.9 1.2 copy-start.8
  328.9 234.9 %reduce-scatter.6.cloned.1.call-start = ((), (), s32[]{:S(2)}) async-start(), calls=%async_computation.11 | async-start | bytes 6127616 | tf_op jit(solution)/shard_map/reduce_scatter | solution.py:113
  337.3 7.4 %slice-start = ((s8[5767168]{0:T(1024)(128)(4,1)}), s8[1572864]{0:T(1024)(128)(4,1)S(1)}, s32[]{:S(2)}) async-start(s8[5767168]{0:T(1024)(128)(4,1)} %bitcast.127), calls=%async_computation.13 | async-start | bytes 3145728
  337.4 7.4 %slice-start.1 = ((s8[5767168]{0:T(1024)(128)(4,1)}), s8[4194304]{0:T(1024)(128)(4,1)S(1)}, s32[]{:S(2)}) async-start(s8[5767168]{0:T(1024)(128)(4,1)} %bitcast.127), calls=%async_computation.14 | async-start | bytes 8388608
  337.4 7.4 %copy-start.9 = (bf16[8,1,48,1408]{3,2,0,1:T(8,128)(2,1)S(1)}, bf16[8,1,48,1408]{3,2,0,1:T(8,128)(2,1)}, u32[]{:S(2)}) copy-start(bf16[8,1,48,1408]{3,2,0,1:T(8,128)(2,1)} %get-tuple-element.22) | copy-start | bytes 3244036
  348.6 25.1 %all-to-all-start.4 = ((bf16[8,48,2048]{2,1,0:T(8,128)(2,1)}), bf16[8,48,2048]{2,1,0:T(8,128)(2,1)S(1)}, u32[]{:S(2)}, u32[]{:S(2)}) async-start(bf16[8,48,2048]{2,1,0:T(8,128)(2,1)} %fusion.31), calls=%async_computation.4 | async-start | bytes 3145728 | tf_op jit(solution)/shard_map/all_to_all | solution.py:95
  373.7 6.6 %copy-start.3 = (bf16[8,48,2048]{2,1,0:T(8,128)(2,1)}, bf16[8,48,2048]{2,1,0:T(8,128)(2,1)S(1)}, u32[]{:S(2)}) copy-start(bf16[8,48,2048]{2,1,0:T(8,128)(2,1)S(1)} %all-to-all-done.4) | copy-start | bytes 4718596
  373.7 36.1 %all-to-all-start.2 = ((bf16[8,48,2048]{2,1,0:T(8,128)(2,1)}), bf16[8,48,2048]{2,1,0:T(8,128)(2,1)S(1)}, u32[]{:S(2)}, u32[]{:S(2)}) async-start(bf16[8,48,2048]{2,1,0:T(8,128)(2,1)} %fusion.28), calls=%async_computation.2 | async-start | bytes 3145728 | tf_op jit(solution)/shard_map/all_to_all | solution.py:61
  417.0 12.0 %copy-start.2 = (f32[256,2048]{1,0:T(8,128)S(1)}, f32[256,2048]{1,0:T(8,128)}, u32[]{:S(2)}) copy-start(f32[256,2048]{1,0:T(8,128)} %convert_element_type.115) | copy-start | bytes 6291460
Sparse Core Ops, SparseCore 0:
  10.1 61.1 all-gather.2
  73.5 58.4 all-gather.4
  320.5 78.1 reduce-scatter.7
  402.0 79.2 reduce-scatter.3
  484.5 79.2 reduce-scatter.5
